TPU v7x, 512 devices: a whole 4x4x16 slice. The times are simulated.
512 devices in a mesh: tile: 32 (over x, y, core), depth: 16 (over z).
Axes of the slice: x: 4, y: 4, z: 16, core: 2. Of those that a mesh axis runs over, the one named last changes fastest.
Arguments:
- estimate: float32 [32, 1024, 1024], P('depth', 'tile'), may hold values from 0.25 to 4
- views: bfloat16 [8, 32, 1024, 1024], P(None, 'depth', 'tile'), may hold values from 0.19921875 to 5
- kernel_x: float32 [8, 31], replicated, may hold values from 0.01 to 1
- kernel_y: float32 [8, 31], replicated, may hold values from 0.01 to 1
- kernel_z: float32 [8, 31], replicated, may hold values from 0.01 to 1
- offsets: int32 [8], replicated, may hold values from 16 to 384
Outputs:
- updated: float32 [32, 1024, 1024], P('depth', 'tile')
All inputs are finite; a program needn't handle non-finite values.
Results may differ from a plain program's by a relative error of at most 0.0007.
Values may be sent and summed in bfloat16 or wider, within the bound.
A program may use at most 128 MiB of HBM per device.

v0:
```python
import jax
import jax.numpy as jnp
from jax import lax
from jax.sharding import PartitionSpec as P


def extended(array, sides, width):
    for axis, dim in sides:
        devices, length = (lax.axis_size(axis), array.shape[dim])
        up = [(i, (i + 1) % devices) for i in range(devices - 1)]
        down = [(j, i) for i, j in up]
        last = lax.slice_in_dim(array, length - width, length, axis=dim)
        initial = lax.slice_in_dim(array, 0, width, axis=dim)
        before = lax.ppermute(last, axis, up)
        after = lax.ppermute(initial, axis, down)
        array = jnp.concatenate([before, array, after], axis=dim)
    return array


def normalize(kernel):
    return kernel / jnp.sum(kernel, axis=1, keepdims=True)


def tap_factor(kernel, tap_index, ndims):
    return kernel[:, tap_index].reshape((kernel.shape[0],) + (1,) * (ndims - 1))


def convolve(values, kernel, axis):
    margin = kernel.shape[1] // 2
    length = values.shape[axis]
    widths = [(0, 0)] * values.ndim
    widths[axis] = (margin, margin)
    padded = jnp.pad(values, widths)
    summed = jnp.zeros_like(values)
    for tap_index in range(kernel.shape[1]):
        summed = summed + tap_factor(kernel, tap_index, values.ndim) * lax.slice_in_dim(
            padded, tap_index, tap_index + length, axis=axis
        )
    return summed


def strip_pass(widened, kernel, length, axis):
    shape = list(widened.shape)
    shape[0] = kernel.shape[0]
    shape[axis] = length
    summed = jnp.zeros(tuple(shape), jnp.float32)
    for tap_index in range(kernel.shape[1]):
        summed = summed + tap_factor(kernel, tap_index, widened.ndim) * lax.slice_in_dim(
            widened, tap_index, tap_index + length, axis=axis
        )
    return summed


def shards(estimate, views, kernel_x, kernel_y, kernel_z, offsets):
    kernel_x = normalize(kernel_x)
    kernel_y = normalize(kernel_y)
    kernel_z = normalize(kernel_z)
    flipped_x = kernel_x[:, ::-1]
    flipped_y = kernel_y[:, ::-1]
    flipped_z = kernel_z[:, ::-1]
    margin = kernel_x.shape[1] // 2
    strip_rows = estimate.shape[1]
    slab_rows = strip_rows * lax.axis_size("tile")
    view_rows = 5 * slab_rows // 8
    tile_index = lax.axis_index("tile")
    row_ids = tile_index * strip_rows + jnp.arange(strip_rows, dtype=jnp.int32)
    inside = (row_ids[None, :] >= offsets[:, None]) & (
        row_ids[None, :] < offsets[:, None] + view_rows
    )
    covered = inside.astype(jnp.float32)
    coverage = jnp.sum(covered, axis=0)
    widened = extended(estimate.astype(jnp.bfloat16), (("tile", 1),), margin).astype(estimate.dtype)
    partial_blur = strip_pass(widened[None], kernel_x, strip_rows, 2)
    partial_blur = convolve(partial_blur, kernel_y, 3)
    deepened = lax.all_to_all(
        partial_blur.astype(jnp.bfloat16), "depth", split_axis=2, concat_axis=1, tiled=True
    ).astype(partial_blur.dtype)
    blurred_deep = convolve(deepened, kernel_z, 1)
    blurred = lax.all_to_all(
        blurred_deep.astype(jnp.bfloat16), "depth", split_axis=1, concat_axis=2, tiled=True
    ).astype(blurred_deep.dtype)
    correction = covered[:, None, :, None] * (views.astype(jnp.float32) / blurred - 1.0)
    correction_deep = lax.all_to_all(
        correction.astype(jnp.bfloat16), "depth", split_axis=2, concat_axis=1, tiled=True
    ).astype(correction.dtype)
    backward_deep = convolve(correction_deep, flipped_z, 1)
    backward = lax.all_to_all(
        backward_deep.astype(jnp.bfloat16), "depth", split_axis=1, concat_axis=2, tiled=True
    ).astype(backward_deep.dtype)
    backward = convolve(backward, flipped_y, 3)
    widened_back = extended(backward.astype(jnp.bfloat16), (("tile", 2),), margin).astype(
        backward.dtype
    )
    summed = jnp.sum(strip_pass(widened_back, flipped_x, strip_rows, 2), axis=0)
    return estimate * (1.0 + summed / jnp.maximum(coverage, 1.0)[None, :, None])


def solution(mesh):
    in_specs = (P("depth", "tile", None), P(None, "depth", "tile", None), P(), P(), P(), P())
    out_specs = P("depth", "tile", None)
    return jax.shard_map(shards, mesh=mesh, in_specs=in_specs, out_specs=out_specs, check_vma=False)
```

profile of v0, /device:TPU:25, one launch (start us, length us, event | category | flops | bytes accessed | tf_op | source)
XLA Modules:
  0.0 338.1 jit_solution(16546298350082343880)
XLA Ops:
  0.0 1.0 convert_element_type.97
  1.0 3.3 collective-permute-start
  4.3 1.9 collective-permute-start.1
  6.3 1.0 convert_bitcast_fusion.4
  7.2 0.8 reduce_sum.45
  8.0 0.8 broadcast_divide_fusion.2
  8.8 0.5 slice_reduce_fusion.92
  9.7 0.8 reduce_sum.46
  10.5 0.8 broadcast_divide_fusion.1
  11.2 0.5 slice_reduce_fusion.91
  12.2 0.6 slice_bitcast_fusion.30
  13.2 4.6 %multiply_add_fusion = f32[8,2,32,1024]{3,0,2,1:T(8,128)S(1)} fusion(f32[2,32,1024]{2,1,0:T(8,128)S(1)} %get-tuple-element.101, f32[2,32,1024]{2,1,0:T(8,128)S(1)} %get-tuple-element.102, f32[8]{0:T(128)S(1)} %get-tuple-element.68, f32[2,32,1024]{2,1,0:T(8,128)S(1)} %get-tuple-element.103, f32[8]{0:T(128)S(1)} %get-tuple-element.69, ...), kind=kLoop, calls=%fused_computation.431 | loop fusion | flops 31981568 | bytes 10224608 | tf_op jit(solution)/shard_map/add | solution.py:48
  17.9 16.7 %fusion.54 = bf16[8,2,32,1024]{3,0,2,1:T(8,128)(2,1)S(1)} fusion(f32[8,2,32,1024]{3,0,2,1:T(8,128)S(1)} %multiply_add_fusion, f32[8]{0:T(128)S(1)} %get-tuple-element.37, f32[8]{0:T(128)S(1)} %get-tuple-element.38, f32[8]{0:T(128)S(1)} %get-tuple-element.39, f32[8]{0:T(128)S(1)} %get-tuple-element.40, f32[8]{0:T(128)S(1)} %get-tuple-element.41, ...), kind=kLoop, calls=%fused_computation.174 | loop fusion | flops 32505856 | bytes 3146720 | tf_op jit(solution)/shard_map/convert_element_type | solution.py:76
  34.6 1.1 copy.23
  35.7 14.9 %all-to-all-start = ((bf16[8,2,32,1024]{3,0,1,2:T(8,128)(2,1)}), bf16[8,2,32,1024]{3,0,1,2:T(8,128)(2,1)S(1)}, u32[]{:S(2)}, u32[]{:S(2)}) async-start(bf16[8,2,32,1024]{3,0,1,2:T(8,128)(2,1)} %copy.23), calls=%async_computation | async-start | bytes 2097152 | tf_op jit(solution)/shard_map/all_to_all | solution.py:75
  51.2 0.5 slice_reduce_fusion.90
  51.7 43.3 %all-to-all-done = bf16[8,2,32,1024]{3,0,1,2:T(8,128)(2,1)S(1)} async-done(((bf16[8,2,32,1024]{3,0,1,2:T(8,128)(2,1)}), bf16[8,2,32,1024]{3,0,1,2:T(8,128)(2,1)S(1)}, u32[]{:S(2)}, u32[]{:S(2)}) %all-to-all-start) | async-done | bytes 1048608 | tf_op jit(solution)/shard_map/all_to_all | solution.py:75
  95.5 7.6 %fusion.175 = bf16[8,32,2,1024]{3,0,2,1:T(8,128)(2,1)} fusion(f32[8,32,2,1024]{3,0,2,1:T(8,128)S(1)} %bitcast.88, f32[8]{0:T(128)S(1)} %get-tuple-element.6, f32[8]{0:T(128)S(1)} %get-tuple-element.7, f32[8]{0:T(128)S(1)} %get-tuple-element.8, f32[8]{0:T(128)S(1)} %get-tuple-element.9, f32[8]{0:T(128)S(1)} %get-tuple-element.10, ...), kind=kLoop, calls=%fused_computation.295 | loop fusion | flops 32505856 | bytes 3146720 | tf_op jit(solution)/shard_map/convert_element_type | solution.py:80
  103.1 13.7 %all-to-all-start.1 = ((bf16[8,32,2,1024]{3,0,2,1:T(8,128)(2,1)}), bf16[8,32,2,1024]{3,0,2,1:T(8,128)(2,1)S(1)}, u32[]{:S(2)}, u32[]{:S(2)}) async-start(bf16[8,32,2,1024]{3,0,2,1:T(8,128)(2,1)} %fusion.175), calls=%async_computation.1 | async-start | bytes 2097152 | tf_op jit(solution)/shard_map/all_to_all | solution.py:79
  117.0 45.0 %all-to-all-done.1 = bf16[8,32,2,1024]{3,0,2,1:T(8,128)(2,1)S(1)} async-done(((bf16[8,32,2,1024]{3,0,2,1:T(8,128)(2,1)}), bf16[8,32,2,1024]{3,0,2,1:T(8,128)(2,1)S(1)}, u32[]{:S(2)}, u32[]{:S(2)}) %all-to-all-start.1) | async-done | bytes 1048608 | tf_op jit(solution)/shard_map/all_to_all | solution.py:79
  162.5 1.0 copy-done.1
  163.5 0.8 multiply_convert_fusion
  164.4 57.9 %all_to_all.16 = bf16[8,2,32,1024]{3,0,1,2:T(8,128)(2,1)S(1)} all-to-all(bf16[8,2,32,1024]{3,0,1,2:T(8,128)(2,1)S(1)} %copy.27), channel_id=1, replica_groups=mesh['tile'=32,'depth'=16] {'depth'}, dimensions={2} | all-to-all | bytes 2097152 | tf_op jit(solution)/shard_map/all_to_all | solution.py:83
  222.8 6.9 %fusion.236 = bf16[8,32,2,1024]{3,0,2,1:T(8,128)(2,1)S(1)} fusion(f32[8,32,2,1024]{3,0,2,1:T(8,128)S(1)} %bitcast.86, f32[8]{0:T(128)S(1)} %get-tuple-element.6, f32[8]{0:T(128)S(1)} %get-tuple-element.7, f32[8]{0:T(128)S(1)} %get-tuple-element.8, f32[8]{0:T(128)S(1)} %get-tuple-element.9, f32[8]{0:T(128)S(1)} %get-tuple-element.10, ...), kind=kLoop, calls=%fused_computation.356 | loop fusion | flops 32505856 | bytes 3146720 | tf_op jit(solution)/shard_map/convert_element_type | solution.py:88
  229.7 57.8 %all_to_all.17 = bf16[8,32,2,1024]{3,0,2,1:T(8,128)(2,1)S(1)} all-to-all(bf16[8,32,2,1024]{3,0,2,1:T(8,128)(2,1)S(1)} %fusion.236), channel_id=1, replica_groups=mesh['tile'=32,'depth'=16] {'depth'}, dimensions={1} | all-to-all | bytes 2097152 | tf_op jit(solution)/shard_map/all_to_all | solution.py:87
  288.1 16.7 %fusion.115 = bf16[8,2,32,1024]{3,0,2,1:T(8,128)(2,1)S(1)} fusion(f32[8,2,32,1024]{3,0,2,1:T(8,128)S(1)} %bitcast.87, f32[8]{0:T(128)S(1)} %get-tuple-element.37, f32[8]{0:T(128)S(1)} %get-tuple-element.38, f32[8]{0:T(128)S(1)} %get-tuple-element.39, f32[8]{0:T(128)S(1)} %get-tuple-element.40, f32[8]{0:T(128)S(1)} %get-tuple-element.41, ...), kind=kLoop, calls=%fused_computation.235 | loop fusion | flops 32505856 | bytes 3146720 | tf_op jit(solution)/shard_map/convert_element_type | solution.py:91
  304.9 9.5 %collective-permute-start.2 = (bf16[8,2,15,1024]{3,0,2,1:T(8,128)(2,1)S(1)}, bf16[8,2,15,1024]{3,0,2,1:T(8,128)(2,1)S(1)}, u32[]{:S(2)}, u32[]{:S(2)}) collective-permute-start(bf16[8,2,15,1024]{3,0,2,1:T(8,128)(2,1)S(1)} %get-tuple-element.98), channel_id=1, source_target_pairs={{0,16},{16,32},{32,48},{48,64},{64,80},{80,96},{96,112},{112,128},... | collective-permute-start | bytes 1474568 | tf_op jit(solution)/shard_map/ppermute | solution.py:14
  314.4 1.9 collective-permute-start.3
  316.4 3.7 %collective-permute-done.2 = bf16[8,2,15,1024]{3,0,2,1:T(8,128)(2,1)S(1)} collective-permute-done((bf16[8,2,15,1024]{3,0,2,1:T(8,128)(2,1)S(1)}, bf16[8,2,15,1024]{3,0,2,1:T(8,128)(2,1)S(1)}, u32[]{:S(2)}, u32[]{:S(2)}) %collective-permute-start.2) | collective-permute-done | bytes 491552 | tf_op jit(solution)/shard_map/ppermute | solution.py:14
  320.1 6.5 %collective-permute-done.3 = bf16[8,2,15,1024]{3,0,2,1:T(8,128)(2,1)S(1)} collective-permute-done((bf16[8,2,15,1024]{3,0,2,1:T(8,128)(2,1)S(1)}, bf16[8,2,15,1024]{3,0,2,1:T(8,128)(2,1)S(1)}, u32[]{:S(2)}, u32[]{:S(2)}) %collective-permute-start.3) | collective-permute-done | bytes 491552 | tf_op jit(solution)/shard_map/ppermute | solution.py:15
  326.9 10.3 %fusion.245 = f32[2,32,1024]{2,1,0:T(8,128)S(1)} fusion(f32[8,2,62,1024]{3,0,2,1:T(8,128)S(1)} %maximum_convert_fusion, f32[8]{0:T(128)S(1)} %get-tuple-element.68, f32[8]{0:T(128)S(1)} %get-tuple-element.69, f32[8]{0:T(128)S(1)} %get-tuple-element.70, f32[8]{0:T(128)S(1)} %get-tuple-element.71, f32[8]{0:T(128)S(1)} %get-tuple-element.72, ...), kind=kLoop, calls=%fused_computation.366 | loop fusion | flops 32440320 | bytes 65274848 | tf_op jit(solution)/shard_map/reduce_sum | solution.py:94
  337.3 0.8 add_multiply_fusion
  (36 shorter events, 4.4 us)
Async XLA Ops:
  1.0 11.1 %collective-permute-start = (bf16[2,15,1024]{2,1,0:T(8,128)(2,1)S(1)}, bf16[2,15,1024]{2,1,0:T(8,128)(2,1)S(1)}, u32[]{:S(2)}, u32[]{:S(2)}) collective-permute-start(bf16[2,15,1024]{2,1,0:T(8,128)(2,1)S(1)} %get-tuple-element.131), channel_id=1, source_target_pairs={{0,16},{16,32},{32,48},{48,64},{64,80},{80,96},{96,112},{112,128},... | collective-permute-start | bytes 184328 | tf_op jit(solution)/shard_map/ppermute | solution.py:14
  4.3 7.8 %collective-permute-start.1 = (bf16[2,15,1024]{2,1,0:T(8,128)(2,1)S(1)}, bf16[2,15,1024]{2,1,0:T(8,128)(2,1)S(1)}, u32[]{:S(2)}, u32[]{:S(2)}) collective-permute-start(bf16[2,15,1024]{2,1,0:T(8,128)(2,1)S(1)} %get-tuple-element.132), channel_id=1, source_target_pairs={{16,0},{32,16},{48,32},{64,48},{80,64},{96,80},{112,96},{128,112},... | collective-permute-start | bytes 184328 | tf_op jit(solution)/shard_map/ppermute | solution.py:15
  34.6 16.0 %copy-start.2 = (f32[8,31]{1,0:T(8,128)S(1)}, f32[8,31]{1,0:T(8,128)}, u32[]{:S(2)}) copy-start(f32[8,31]{1,0:T(8,128)} %param.10) | copy-start | bytes 2980
  35.7 59.3 %all-to-all-start = ((bf16[8,2,32,1024]{3,0,1,2:T(8,128)(2,1)}), bf16[8,2,32,1024]{3,0,1,2:T(8,128)(2,1)S(1)}, u32[]{:S(2)}, u32[]{:S(2)}) async-start(bf16[8,2,32,1024]{3,0,1,2:T(8,128)(2,1)} %copy.23), calls=%async_computation | async-start | bytes 2097152 | tf_op jit(solution)/shard_map/all_to_all | solution.py:75
  95.5 21.3 %copy-start.3 = (s32[8]{0:T(128)S(1)}, s32[8]{0:T(128)}, u32[]{:S(2)}) copy-start(s32[8]{0:T(128)} %param.11) | copy-start | bytes 100
  103.1 58.9 %all-to-all-start.1 = ((bf16[8,32,2,1024]{3,0,2,1:T(8,128)(2,1)}), bf16[8,32,2,1024]{3,0,2,1:T(8,128)(2,1)S(1)}, u32[]{:S(2)}, u32[]{:S(2)}) async-start(bf16[8,32,2,1024]{3,0,2,1:T(8,128)(2,1)} %fusion.175), calls=%async_computation.1 | async-start | bytes 2097152 | tf_op jit(solution)/shard_map/all_to_all | solution.py:79
  162.3 1.2 copy-start.1
  304.9 15.2 %collective-permute-start.2 = (bf16[8,2,15,1024]{3,0,2,1:T(8,128)(2,1)S(1)}, bf16[8,2,15,1024]{3,0,2,1:T(8,128)(2,1)S(1)}, u32[]{:S(2)}, u32[]{:S(2)}) collective-permute-start(bf16[8,2,15,1024]{3,0,2,1:T(8,128)(2,1)S(1)} %get-tuple-element.98), channel_id=1, source_target_pairs={{0,16},{16,32},{32,48},{48,64},{64,80},{80,96},{96,112},{112,128},... | collective-permute-start | bytes 1474568 | tf_op jit(solution)/shard_map/ppermute | solution.py:14
  314.4 12.3 %collective-permute-start.3 = (bf16[8,2,15,1024]{3,0,2,1:T(8,128)(2,1)S(1)}, bf16[8,2,15,1024]{3,0,2,1:T(8,128)(2,1)S(1)}, u32[]{:S(2)}, u32[]{:S(2)}) collective-permute-start(bf16[8,2,15,1024]{3,0,2,1:T(8,128)(2,1)S(1)} %get-tuple-element.99), channel_id=1, source_target_pairs={{16,0},{32,16},{48,32},{64,48},{80,64},{96,80},{112,96},{128,112},... | collective-permute-start | bytes 1474568 | tf_op jit(solution)/shard_map/ppermute | solution.py:15
  326.9 10.3 %copy-start = (f32[2,32,1024]{2,1,0:T(8,128)S(1)}, f32[2,32,1024]{2,1,0:T(8,128)}, u32[]{:S(2)}) copy-start(f32[2,32,1024]{2,1,0:T(8,128)} %param.6) | copy-start | bytes 786436
where the time goes:
time: 339 us; the launch traced here: 338 us
  blocking collectives  116 us (34%)
  waiting for transfers between devices  98.6 us (29%)
  other arithmetic  71.4 us (21%)
  starting transfers between devices  45.2 us (13%)
  local copies, waits for them, and re-layouts  6.82 us (2%)
    all_to_all x1, blocking collectives, shards(): lax.all_to_all(correction.astype(jnp.bfloat16), 'depth', split_axis=2, co...  57.9 us
    all_to_all x1, blocking collectives, shards(): lax.all_to_all(backward_deep.astype(jnp.bfloat16), 'depth', split_axis=1,...  57.8 us
    all_to_all x1, waiting for transfers between devices, shards(): lax.all_to_all(blurred_deep.astype(jnp.bfloat16), 'depth', split_axis=1,...  45 us
    all_to_all x1, waiting for transfers between devices, shards(): lax.all_to_all(partial_blur.astype(jnp.bfloat16), 'depth', split_axis=2,...  43.3 us
    convert_element_type x1, other arithmetic, shards(): backward.astype(jnp.bfloat16)  16.7 us
    convert_element_type x1, other arithmetic, shards(): partial_blur.astype(jnp.bfloat16)  16.7 us
    all_to_all x1, starting transfers between devices, shards(): lax.all_to_all(partial_blur.astype(jnp.bfloat16), 'depth', split_axis=2,...  14.9 us
    all_to_all x1, starting transfers between devices, shards(): lax.all_to_all(blurred_deep.astype(jnp.bfloat16), 'depth', split_axis=1,...  13.7 us
  transfers between devices with their start and end apart: 6, of which 4 were waited for; matrix products, arithmetic and copies ran while one was open for 2% of the time, Pallas kernels for 0%

commit v1 on v0

v1 whole, which is shorter than its diff:
```python
import jax
import jax.numpy as jnp
from jax import lax
from jax.experimental import pallas as pl
from jax.experimental.pallas import tpu as pltpu
from jax.sharding import PartitionSpec as P

MESH = pl.DeviceIdType.MESH
BF = jnp.bfloat16
F32 = jnp.float32
V = 8
T = 31
R = 32
H = 16
RH = R + 2 * H
NC = 1024
PAD = 128
CT = 256


def place(way, hop):
    if hop == 0:
        return 0, 0
    if hop == 8:
        return 0, 1
    return hop, way


def body(
    est, views, kx, ky, kz, offs, out,
    gath, acc, blur, corr, back, amat, bmat, xfwd, xbwd, yfwd, ybwd, vbuf, part, own, sbuf, rbuf,
    g_send, g_recv, h_send, h_recv, v_sem, y_send, y_recv, r_send, r_recv,
):
    b = lax.axis_index("depth")
    t = lax.axis_index("tile")
    nz = lax.axis_size("depth")
    nt = lax.axis_size("tile")
    rows_total = R * nt
    view_rows = 5 * rows_total // 8
    zr = lax.rem(b + 1, nz)
    zl = lax.rem(b + nz - 1, nz)
    tu = lax.rem(t + nt - 1, nt)
    td = lax.rem(t + 1, nt)
    z_to = ((t, zr), (t, zl))
    t_to = ((tu, b), (td, b))

    barrier = pltpu.get_barrier_semaphore()
    corners = tuple((x, z) for x in (tu, td) for z in (zr, zl))
    for device in z_to + t_to + corners:
        pl.semaphore_signal(barrier, inc=1, device_id=device, device_id_type=MESH)
    vcopy = pltpu.make_async_copy(views, vbuf, v_sem)
    vcopy.start()
    gath[0, 0, :, H : H + R, :] = est[...].astype(BF)

    def hop_copy(way, hop, q, k):
        pair, side = place(way, hop)
        pair2, side2 = place(way, hop + 1)
        return pltpu.make_async_remote_copy(
            src_ref=gath.at[pair, side, q, pl.ds(H + k * H, H), :],
            dst_ref=gath.at[pair2, side2, q, pl.ds(H + k * H, H), :],
            send_sem=g_send.at[way, hop, q, k],
            recv_sem=g_recv.at[way, hop, q, k],
            device_id=z_to[way],
            device_id_type=MESH,
        )

    def halo_copy(pair, side, q, k):
        src, dst = ((H, H + R), (R, 0))[k]
        pair2, side2, device = pair, side, t_to[k]
        if (pair, side) == (0, 1):
            way = 1 - q
            pair2, side2 = place(way, 7)
            device = ((tu, td)[k], (zr, zl)[way])
        return pltpu.make_async_remote_copy(
            src_ref=gath.at[pair2, side2, q, pl.ds(src, H), :],
            dst_ref=gath.at[pair, side, q, pl.ds(dst, H), :],
            send_sem=h_send.at[pair, side, q, k],
            recv_sem=h_recv.at[pair, side, q, k],
            device_id=device,
            device_id_type=MESH,
        )

    pl.semaphore_wait(barrier, 8)
    planes = ((1, 0), (0, 1))
    pieces = ((0, 0), (0, 1), (1, 0), (1, 1))
    for i, k in pieces:
        for way in range(2):
            hop_copy(way, 0, planes[way][i], k).start()
    for q in range(2):
        for k in range(2):
            halo_copy(0, 0, q, k).start()

    lane = lax.broadcasted_iota(jnp.int32, (R, 2 * RH), 1)
    low = lane < RH
    src_row = jnp.where(low, lane, lane - RH)
    diff = src_row - lax.broadcasted_iota(jnp.int32, (R, 2 * RH), 0) - 1
    row_at = src_row + (t * R - H)
    exists = (row_at >= 0) & (row_at < rows_total)
    gap = lax.broadcasted_iota(jnp.int32, (PAD, PAD), 0) - lax.broadcasted_iota(jnp.int32, (PAD, PAD), 1)
    ring = jnp.where(gap + 15 < 0, gap + 15 + PAD, jnp.where(gap + 15 >= PAD, gap + 15 - PAD, gap + 15))

    def tables(v, carry):
        sx = kx[v, 0]
        sy = ky[v, 0]
        sz = kz[v, 0]
        for j in range(1, T):
            sx = sx + kx[v, j]
            sy = sy + ky[v, j]
            sz = sz + kz[v, j]
        xf = jnp.zeros((R, 2 * RH), F32)
        xb = jnp.zeros((R, 2 * RH), F32)
        cf = jnp.zeros((PAD, PAD), F32)
        cb = jnp.zeros((PAD, PAD), F32)
        for j in range(T):
            hit = diff == j
            xf = jnp.where(hit, kx[v, j], xf)
            xb = jnp.where(hit, kx[v, T - 1 - j], xb)
            hit = ring == j
            cf = jnp.where(hit, ky[v, j], cf)
            cb = jnp.where(hit, ky[v, T - 1 - j], cb)
        scale = jnp.full((R, 2 * RH), sx * sz, F32)
        xfwd[v] = jnp.where(exists, xf / scale, 0.0)
        xbwd[v] = jnp.where(exists, xb / scale, 0.0)
        for ref, c in ((yfwd, cf), (ybwd, cb)):
            c = c / jnp.full((PAD, PAD), sy, F32)
            bands = (
                jnp.where(gap >= PAD - 15, c, 0.0).astype(BF),
                jnp.where((gap <= 15) & (gap >= -15), c, 0.0).astype(BF),
                jnp.where(gap <= 15 - PAD, c, 0.0).astype(BF),
            )
            none = jnp.zeros((PAD, PAD), BF)
            for i in range(4):
                for j in range(2):
                    ref[v, PAD * i : PAD * (i + 1), PAD * j : PAD * (j + 1)] = bands[i - j] if 0 <= i - j < 3 else none
        return carry

    lax.fori_loop(0, V, tables, 0)

    def mats(pair):
        offsets = (0, 8) if pair == 0 else (-pair, pair)
        zs = [2 * lax.rem(b + o + nz, nz) - 2 * b + 15 for o in offsets]

        def one(v, carry):
            xf = xfwd[v]
            xb = xbwd[v]
            c = {}
            for side in range(2):
                for q in range(2):
                    for p in range(2):
                        at = zs[side] + (q - p)
                        ok = (at >= 0) & (at < T)
                        c[side, q, p] = jnp.where(ok, kz[v, jnp.clip(at, 0, T - 1)], 0.0)
            for side in range(2):
                for p in range(2):
                    z = jnp.where(low, c[side, 0, p], c[side, 1, p])
                    amat[pair, pl.ds(pl.multiple_of(v * 64 + p * R, R), R), side * 128 : side * 128 + 128] = (xf * z).astype(BF)
                for q in range(2):
                    z = jnp.where(low, c[side, q, 0], c[side, q, 1])
                    first = side * 64 + q * R
                    bmat[pair, first : first + R, pl.ds(pl.multiple_of(v * 128, 128), 128)] = (xb * z).astype(BF)
            return carry

        lax.fori_loop(0, V, one, 0)

    def forward(pair, begin, end):
        def one(n, carry):
            cols = pl.ds(pl.multiple_of(n * CT, CT), CT)
            block = gath[pair, :, :, :, cols].reshape(4 * RH, CT)
            got = jnp.dot(amat[pair], block, preferred_element_type=F32)
            if not begin:
                got = got + acc[:, cols]
            if end:
                blur[:, pl.ds(pl.multiple_of(n * CT + PAD, PAD), CT)] = got.astype(BF)
            else:
                acc[:, cols] = got
            return carry

        lax.fori_loop(0, NC // CT, one, 0)

    for ref in (blur, corr):
        ref[:, :PAD] = jnp.zeros((ref.shape[0], PAD), BF)
        ref[:, PAD + NC :] = jnp.zeros((ref.shape[0], PAD), BF)

    def halos(pair, side):
        for q in range(2):
            for k in range(2):
                halo_copy(pair, side, q, k).wait_recv()

    for hop in range(1, 8):
        for i, k in pieces:
            for way in range(2):
                q = planes[way][i]
                hop_copy(way, hop - 1, q, k).wait_recv()
                if hop < 7 or i == 0:
                    hop_copy(way, hop, q, k).start()
                if hop == 7 and i == 0:
                    halo_copy(0, 1, q, k).start()
        for side in range(2):
            for q in range(2):
                for k in range(2):
                    halo_copy(hop, side, q, k).start()
        mats(hop)
        if hop >= 2:
            for side in range(2):
                halos(hop - 1, side)
            forward(hop - 1, hop == 2, False)
    mats(0)
    for side in range(2):
        halos(7, side)
    forward(7, False, False)
    for k in range(2):
        for way in range(2):
            hop_copy(way, 7, planes[way][0], k).wait_recv()
    for side in range(2):
        halos(0, side)
    forward(0, False, True)
    vcopy.wait()

    row = lax.broadcasted_iota(jnp.int32, (2 * R, CT), 0)
    row = jnp.where(row >= R, row - R, row) + t * R

    def y_copy(v, k):
        src, dst = ((H, H + R), (R, 0))[k]
        return pltpu.make_async_remote_copy(
            src_ref=back.at[v, :, pl.ds(src, H), :],
            dst_ref=back.at[v, :, pl.ds(dst, H), :],
            send_sem=y_send.at[v, k],
            recv_sem=y_recv.at[v, k],
            device_id=t_to[k],
            device_id_type=MESH,
        )

    def view_step(v, carry):
        inside = (row >= offs[v]) & (row < offs[v] + view_rows)
        rows = pl.ds(pl.multiple_of(v * 64, 64), 64)
        lhs = jnp.concatenate([blur[rows, n * CT : n * CT + 2 * CT] for n in range(4)], axis=0)
        blurred = jnp.dot(lhs, yfwd[v], preferred_element_type=F32)
        for n in range(4):
            seen = vbuf[v, :, :, n * CT : (n + 1) * CT].astype(F32).reshape(2 * R, CT)
            ratio = seen / blurred[n * 64 : (n + 1) * 64]
            corr[:, PAD + n * CT : PAD + (n + 1) * CT] = jnp.where(inside, ratio - 1.0, 0.0).astype(BF)
        lhs = jnp.concatenate([corr[:, n * CT : n * CT + 2 * CT] for n in range(4)], axis=0)
        spread = jnp.dot(lhs, ybwd[v], preferred_element_type=F32).astype(BF)
        for n in range(4):
            back[v, :, H : H + R, n * CT : (n + 1) * CT] = spread[n * 64 : (n + 1) * 64].reshape(2, R, CT)
        for k in range(2):
            y_copy(v, k).start()
        return carry

    lax.fori_loop(0, V, view_step, 0)

    def y_wait(v, carry):
        for k in range(2):
            y_copy(v, k).wait_recv()
        return carry

    def sum_copy(way, step, piece):
        tiles = pl.ds(0 if piece == 0 else 1 + 8 * piece, 9 if piece == 0 else 8)
        return pltpu.make_async_remote_copy(
            src_ref=sbuf.at[way, step, tiles],
            dst_ref=rbuf.at[way, step, tiles],
            send_sem=r_send.at[way, step, piece],
            recv_sem=r_recv.at[way, step, piece],
            device_id=z_to[way],
            device_id_type=MESH,
        )

    early = 6

    def project(pair, target, first, last):
        def one(n, carry):
            cols = pl.ds(pl.multiple_of(n * CT, CT), CT)
            block = back[first:last, :, :, cols].reshape((last - first) * 2 * RH, CT)
            got = jnp.dot(bmat[pair, :, first * 128 : last * 128], block, preferred_element_type=F32)
            if first:
                got = got + target[:, cols]
            target[:, cols] = got
            return carry

        lax.fori_loop(0, NC // CT, one, 0)

    def message(source, way, step, piece, plane_order):
        i, k = pieces[piece]
        q = plane_order[i]
        at = (64 if step == 0 else (1 - way) * 64) + q * R + k * H
        tiles = [source[at : at + H, 128 * j : 128 * (j + 1)] for j in range(8)]
        if step > 1 or (step == 1 and i == 0):
            sum_copy(way, step - 1, piece).wait_recv()
            base = rbuf[way, step - 1, 0].astype(F32)
            tiles = [tiles[j] + (rbuf[way, step - 1, 1 + 8 * piece + j].astype(F32) + base) for j in range(8)]
        if piece == 0:
            mean = sum(tiles[1:], tiles[0]) * 0.125
            sbuf[way, step, 0] = mean.astype(BF)
        mean = sbuf[way, step, 0].astype(F32)
        for j in range(8):
            sbuf[way, step, 1 + 8 * piece + j] = (tiles[j] - mean).astype(BF)
        sum_copy(way, step, piece).start()

    orders = ((0, 1), (1, 0))
    lax.fori_loop(0, early, y_wait, 0)
    project(0, own, 0, early)
    project(7, part, 0, early)
    lax.fori_loop(early, V, y_wait, 0)
    project(0, own, early, V)
    for piece in range(2):
        for way in range(2):
            message(own, way, 0, piece, orders[way])
    for step in range(1, 8):
        if step == 1:
            project(7, part, early, V)
        else:
            project(8 - step, part, 0, V)
        for piece in range(4):
            for way in range(2):
                message(part, way, step, piece, orders[way])
    rid = lax.broadcasted_iota(jnp.int32, (R, 128), 0) + t * R
    seen_by = jnp.zeros((R, 128), F32)
    for v in range(V):
        seen_by = seen_by + jnp.where((rid >= offs[v]) & (rid < offs[v] + view_rows), 1.0, 0.0)
    share = 1.0 / jnp.maximum(seen_by, 1.0)
    for piece in range(4):
        i, k = pieces[piece]
        for way in range(2):
            sum_copy(way, 7, piece).wait_recv()
            q = orders[way][i]
            base = rbuf[way, 7, 0].astype(F32)
            for j in range(8):
                at = (q * R + k * H, q * R + (k + 1) * H)
                cols = slice(128 * j, 128 * (j + 1))
                own[at[0] : at[1], cols] = own[at[0] : at[1], cols] + (rbuf[way, 7, 1 + 8 * piece + j].astype(F32) + base)
    for q in range(2):
        for j in range(8):
            cols = slice(128 * j, 128 * (j + 1))
            out[q, :, cols] = est[q, :, cols] * (1.0 + own[q * R : (q + 1) * R, cols] * share)

    for hop in range(8):
        for way in range(2):
            for piece in range(4):
                i, k = pieces[piece]
                if hop < 7 or i == 0:
                    hop_copy(way, hop, planes[way][i], k).wait_send()
                if hop > 0 or i == 0:
                    sum_copy(way, hop, piece).wait_send()
        for side in range(2):
            for q in range(2):
                for k in range(2):
                    halo_copy(hop, side, q, k).wait_send()
    for v in range(V):
        for k in range(2):
            y_copy(v, k).wait_send()


def shards(estimate, views, kernel_x, kernel_y, kernel_z, offsets):
    smem = pl.BlockSpec(memory_space=pltpu.SMEM)
    vmem = pl.BlockSpec(memory_space=pltpu.VMEM)
    dma = pltpu.SemaphoreType.DMA
    return pl.pallas_call(
        body,
        out_shape=jax.ShapeDtypeStruct(estimate.shape, F32),
        in_specs=[vmem, pl.BlockSpec(memory_space=pl.ANY), smem, smem, smem, smem],
        out_specs=vmem,
        scratch_shapes=[
            pltpu.VMEM((8, 2, 2, RH, NC), BF),
            pltpu.VMEM((V * 64, NC), F32),
            pltpu.VMEM((V * 64, NC + 2 * PAD), BF),
            pltpu.VMEM((64, NC + 2 * PAD), BF),
            pltpu.VMEM((V, 2, RH, NC), BF),
            pltpu.VMEM((8, V * 64, 256), BF),
            pltpu.VMEM((8, 128, V * 128), BF),
            pltpu.VMEM((V, R, 128), F32),
            pltpu.VMEM((V, R, 128), F32),
            pltpu.VMEM((V, 512, 256), BF),
            pltpu.VMEM((V, 512, 256), BF),
            pltpu.VMEM((V, 2, R, NC), BF),
            pltpu.VMEM((128, NC), F32),
            pltpu.VMEM((128, NC), F32),
            pltpu.VMEM((2, 8, 33, H, 128), BF),
            pltpu.VMEM((2, 8, 33, H, 128), BF),
            dma((2, 8, 2, 2)), dma((2, 8, 2, 2)),
            dma((8, 2, 2, 2)), dma((8, 2, 2, 2)),
            dma,
            dma((V, 2)), dma((V, 2)),
            dma((2, 8, 4)), dma((2, 8, 4)),
        ],
        compiler_params=pltpu.CompilerParams(
            collective_id=0, has_side_effects=True, vmem_limit_bytes=63 * 1024 * 1024
        ),
        name="rl_step",
    )(estimate, views, kernel_x, kernel_y, kernel_z, offsets)


def solution(mesh):
    in_specs = (P("depth", "tile", None), P(None, "depth", "tile", None), P(), P(), P(), P())
    return jax.shard_map(shards, mesh=mesh, in_specs=in_specs, out_specs=P("depth", "tile", None), check_vma=False)
```

time: 339 us -> 96 us (0.28)
  the two profiles are of different devices: /device:TPU:25 before, /device:TPU:32 now
where the time goes in v1:
time: 96 us; the launch traced here: 95.8 us
  Pallas kernels  94.1 us (98%)
  local copies, waits for them, and re-layouts  1.67 us (2%)
    pallas_call x1, Pallas kernels, shards(): pl.pallas_call(body, out_shape=jax.ShapeDtypeStruct(estimate.shape, F32),...  94.1 us

profile of v1, /device:TPU:32, one launch (start us, length us, event | category | flops | bytes accessed | tf_op | source)
XLA Modules:
  0.0 95.8 jit_solution(1961880002414447393)
XLA Ops:
  0.0 94.1 %rl_step.1 = f32[2,32,1024]{2,1,0:T(8,128)} custom-call(f32[2,32,1024]{2,1,0:T(8,128)} %est.1, bf16[8,2,32,1024]{3,2,1,0:T(8,128)(2,1)} %views.1, f32[8,31]{1,0:T(8,128)} %kx.1, f32[8,31]{1,0:T(8,128)} %ky.1, f32[8,31]{1,0:T(8,128)} %kz.1, s32[8]{0:T(128)} %offs.1), custom_call_target="tpu_custom_call" | custom-call | tf_op jit(solution)/shard_map/rl_step/pallas_call | solution.py:357
  94.1 1.7 %copy.8 = f32[2,32,1024]{2,1,0:T(8,128)} copy(f32[2,32,1024]{2,1,0:T(8,128)} %rl_step.1) | data formatting | bytes 524288

commit v2 on v1

v2 whole, which is shorter than its diff:
```python
import jax
import jax.numpy as jnp
from jax import lax
from jax.experimental import pallas as pl
from jax.experimental.pallas import tpu as pltpu
from jax.sharding import PartitionSpec as P

MESH = pl.DeviceIdType.MESH
BF = jnp.bfloat16
F32 = jnp.float32
V = 8
T = 31
R = 32
H = 16
RH = R + 2 * H
NC = 1024
PAD = 128
CT = 256


def place(way, hop):
    if hop == 0:
        return 0, 0
    if hop == 8:
        return 0, 1
    return hop, way


GCOLS = ((0, 768), (768, 1024))
BTILES = ((0, 5), (5, 8))
STILES = ((0, 4), (4, 8))


def body(
    est_in, views, kx_in, ky_in, kz_in, offs_in, out,
    est, kx, ky, kz, offs, obuf, share,
    gath, acc, blur, corr, back, amat, bmat, xfwd, xbwd, yfwd, ybwd, vbuf, part, own, sbuf, rbuf,
    g_send, g_recv, h_send, h_recv, in_sem, o_sem, y_send, y_recv, r_send, r_recv,
):
    b = lax.axis_index("depth")
    t = lax.axis_index("tile")
    nz = lax.axis_size("depth")
    nt = lax.axis_size("tile")
    rows_total = R * nt
    view_rows = 5 * rows_total // 8
    zr = lax.rem(b + 1, nz)
    zl = lax.rem(b + nz - 1, nz)
    tu = lax.rem(t + nt - 1, nt)
    td = lax.rem(t + 1, nt)
    z_to = ((t, zr), (t, zl))
    t_to = ((tu, b), (td, b))

    loads = [
        pltpu.make_async_copy(src, dst, in_sem.at[i])
        for i, (src, dst) in enumerate(
            ((est_in, est), (kx_in, kx), (ky_in, ky), (kz_in, kz), (offs_in, offs), (views, vbuf))
        )
    ]
    for load in loads:
        load.start()
    barrier = pltpu.get_barrier_semaphore()
    corners = tuple((x, z) for x in (tu, td) for z in (zr, zl))
    for device in z_to + t_to + corners:
        pl.semaphore_signal(barrier, inc=1, device_id=device, device_id_type=MESH)

    def hop_copy(way, hop, q, k, c):
        pair, side = place(way, hop)
        pair2, side2 = place(way, hop + 1)
        rows = pl.ds(H + k * H, H) if c == 0 else pl.ds(H, R)
        cols = pl.ds(GCOLS[c][0], GCOLS[c][1] - GCOLS[c][0])
        sem = k if c == 0 else 2
        return pltpu.make_async_remote_copy(
            src_ref=gath.at[pair, side, q, rows, cols],
            dst_ref=gath.at[pair2, side2, q, rows, cols],
            send_sem=g_send.at[way, hop, q, sem],
            recv_sem=g_recv.at[way, hop, q, sem],
            device_id=z_to[way],
            device_id_type=MESH,
        )

    def halo_copy(pair, side, q, k, c):
        src, dst = ((H, H + R), (R, 0))[k]
        cols = pl.ds(GCOLS[c][0], GCOLS[c][1] - GCOLS[c][0])
        if (pair, side) == (0, 1):
            way = 1 - q
            pair2, side2 = place(way, 7)
            device = ((tu, td)[k], (zr, zl)[way])
            source = gath.at[pair2, side2, q, pl.ds(src, H), cols]
            target = gath.at[pair, side, q, pl.ds(dst, H), cols]
        else:
            device = t_to[k]
            source = gath.at[pair, side, :, pl.ds(src, H), cols]
            target = gath.at[pair, side, :, pl.ds(dst, H), cols]
        return pltpu.make_async_remote_copy(
            src_ref=source,
            dst_ref=target,
            send_sem=h_send.at[pair, side, q, k, c],
            recv_sem=h_recv.at[pair, side, q, k, c],
            device_id=device,
            device_id_type=MESH,
        )

    def halo_copies(pair, side, c):
        qs = (0, 1) if (pair, side) == (0, 1) else (0,)
        return [halo_copy(pair, side, q, k, c) for q in qs for k in range(2)]

    planes = ((1, 0), (0, 1))
    pieces = (((0, 0), (0, 1), (1, 0), (1, 1)), ((0, 0), (1, 0)))
    loads[0].wait()
    gath[0, 0, :, H : H + R, :] = est[...].astype(BF)
    pl.semaphore_wait(barrier, 8)
    for c in range(2):
        for i, k in pieces[c]:
            for way in range(2):
                hop_copy(way, 0, planes[way][i], k, c).start()
        for copy in halo_copies(0, 0, c):
            copy.start()
    for load in loads[1:5]:
        load.wait()

    lane = lax.broadcasted_iota(jnp.int32, (R, 2 * RH), 1)
    low = lane < RH
    src_row = jnp.where(low, lane, lane - RH)
    diff = src_row - lax.broadcasted_iota(jnp.int32, (R, 2 * RH), 0) - 1
    row_at = src_row + (t * R - H)
    exists = (row_at >= 0) & (row_at < rows_total)
    gap = lax.broadcasted_iota(jnp.int32, (PAD, PAD), 0) - lax.broadcasted_iota(jnp.int32, (PAD, PAD), 1)
    ring = jnp.where(gap + 15 < 0, gap + 15 + PAD, jnp.where(gap + 15 >= PAD, gap + 15 - PAD, gap + 15))

    def tables(v, carry):
        sx = kx[v, 0]
        sy = ky[v, 0]
        sz = kz[v, 0]
        for j in range(1, T):
            sx = sx + kx[v, j]
            sy = sy + ky[v, j]
            sz = sz + kz[v, j]
        xf = jnp.zeros((R, 2 * RH), F32)
        xb = jnp.zeros((R, 2 * RH), F32)
        cf = jnp.zeros((PAD, PAD), F32)
        cb = jnp.zeros((PAD, PAD), F32)
        for j in range(T):
            hit = diff == j
            xf = jnp.where(hit, kx[v, j], xf)
            xb = jnp.where(hit, kx[v, T - 1 - j], xb)
            hit = ring == j
            cf = jnp.where(hit, ky[v, j], cf)
            cb = jnp.where(hit, ky[v, T - 1 - j], cb)
        scale = jnp.full((R, 2 * RH), sx * sz, F32)
        xfwd[v] = jnp.where(exists, xf / scale, 0.0)
        xbwd[v] = jnp.where(exists, xb / scale, 0.0)
        for ref, c in ((yfwd, cf), (ybwd, cb)):
            c = c / jnp.full((PAD, PAD), sy, F32)
            bands = (
                jnp.where(gap >= PAD - 15, c, 0.0).astype(BF),
                jnp.where((gap <= 15) & (gap >= -15), c, 0.0).astype(BF),
                jnp.where(gap <= 15 - PAD, c, 0.0).astype(BF),
            )
            for i in range(3):
                ref[v, PAD * i : PAD * (i + 1), :] = bands[i]
        return carry

    lax.fori_loop(0, V, tables, 0)

    def mats(pair):
        offsets = (0, 8) if pair == 0 else (-pair, pair)
        zs = [2 * lax.rem(b + o + nz, nz) - 2 * b + 15 for o in offsets]

        def one(v, carry):
            xf = xfwd[v]
            xb = xbwd[v]
            c = {}
            for side in range(2):
                for q in range(2):
                    for p in range(2):
                        at = zs[side] + (q - p)
                        ok = (at >= 0) & (at < T)
                        c[side, q, p] = jnp.where(ok, kz[v, jnp.clip(at, 0, T - 1)], 0.0)
            for side in range(2):
                for p in range(2):
                    z = jnp.where(low, c[side, 0, p], c[side, 1, p])
                    amat[pair, pl.ds(pl.multiple_of(v * 64 + p * R, R), R), side * 128 : side * 128 + 128] = (xf * z).astype(BF)
                for q in range(2):
                    z = jnp.where(low, c[side, q, 0], c[side, q, 1])
                    first = side * 64 + q * R
                    bmat[pair, first : first + R, pl.ds(pl.multiple_of(v * 128, 128), 128)] = (xb * z).astype(BF)
            return carry

        lax.fori_loop(0, V, one, 0)

    def forward(pair, begin, end, chunk):
        def one(n, carry):
            cols = pl.ds(pl.multiple_of(n * CT, CT), CT)
            block = gath[pair, :, :, :, cols].reshape(4 * RH, CT)
            got = jnp.dot(amat[pair], block, preferred_element_type=F32)
            if not begin:
                got = got + acc[:, cols]
            if end:
                blur[:, pl.ds(pl.multiple_of(n * CT + PAD, PAD), CT)] = got.astype(BF)
            else:
                acc[:, cols] = got
            return carry

        lax.fori_loop(GCOLS[chunk][0] // CT, GCOLS[chunk][1] // CT, one, 0)

    for ref in (blur, corr):
        ref[:, :PAD] = jnp.zeros((ref.shape[0], PAD), BF)
        ref[:, PAD + NC :] = jnp.zeros((ref.shape[0], PAD), BF)
    rid = lax.broadcasted_iota(jnp.int32, (R, 128), 0) + t * R
    seen_by = jnp.zeros((R, 128), F32)
    for v in range(V):
        seen_by = seen_by + jnp.where((rid >= offs[v]) & (rid < offs[v] + view_rows), 1.0, 0.0)
    share[...] = 1.0 / jnp.maximum(seen_by, 1.0)

    def halos(pair, c):
        for side in range(2):
            for copy in halo_copies(pair, side, c):
                copy.wait_recv()

    for hop in range(1, 8):
        for c in range(2):
            for i, k in pieces[c]:
                for way in range(2):
                    q = planes[way][i]
                    hop_copy(way, hop - 1, q, k, c).wait_recv()
                    if hop < 7 or i == 0:
                        hop_copy(way, hop, q, k, c).start()
                    if hop == 7 and i == 0:
                        for kk in (k,) if c == 0 else (0, 1):
                            halo_copy(0, 1, q, kk, c).start()
            for side in range(2):
                for copy in halo_copies(hop, side, c):
                    copy.start()
        mats(hop)
        if hop >= 2:
            for c in range(2):
                halos(hop - 1, c)
                forward(hop - 1, hop == 2, False, c)
    mats(0)
    loads[5].wait()

    row = lax.broadcasted_iota(jnp.int32, (2 * R, 128), 0)
    row = jnp.where(row >= R, row - R, row) + t * R

    def y_copy(v, k, c):
        src, dst = ((H, H + R), (R, 0))[k]
        cols = pl.ds(STILES[c][0] * 128, (STILES[c][1] - STILES[c][0]) * 128)
        return pltpu.make_async_remote_copy(
            src_ref=back.at[v, :, pl.ds(src, H), cols],
            dst_ref=back.at[v, :, pl.ds(dst, H), cols],
            send_sem=y_send.at[v, k, c],
            recv_sem=y_recv.at[v, k, c],
            device_id=t_to[k],
            device_id_type=MESH,
        )

    def view_work(v, c):
        inside = (row >= offs[v]) & (row < offs[v] + view_rows)
        rows = pl.ds(pl.multiple_of(v * 64, 64), 64)
        tiles = range(*BTILES[c])
        lhs = jnp.concatenate([blur[rows, n * 128 : n * 128 + 384] for n in tiles], axis=0)
        blurred = jnp.dot(lhs, yfwd[v], preferred_element_type=F32)
        for i, n in enumerate(tiles):
            seen = vbuf[v, :, :, n * 128 : (n + 1) * 128].astype(F32).reshape(2 * R, 128)
            ratio = seen / blurred[i * 64 : (i + 1) * 64]
            corr[rows, PAD + n * 128 : PAD + (n + 1) * 128] = jnp.where(inside, ratio - 1.0, 0.0).astype(BF)
        tiles = range(*STILES[c])
        lhs = jnp.concatenate([corr[rows, n * 128 : n * 128 + 384] for n in tiles], axis=0)
        spread = jnp.dot(lhs, ybwd[v], preferred_element_type=F32).astype(BF)
        for i, n in enumerate(tiles):
            back[v, :, H : H + R, n * 128 : (n + 1) * 128] = spread[i * 64 : (i + 1) * 64].reshape(2, R, 128)

    def view_step(c):
        def step(i, carry):
            for v in (2 * i, 2 * i + 1):
                view_work(v, c)
            for v in (2 * i, 2 * i + 1):
                for k in range(2):
                    y_copy(v, k, c).start()
            return carry

        lax.fori_loop(0, V // 2, step, 0)

    for c in range(2):
        halos(7, c)
        forward(7, False, False, c)
        for i, k in pieces[c]:
            if i == 0:
                for way in range(2):
                    hop_copy(way, 7, planes[way][0], k, c).wait_recv()
        halos(0, c)
        forward(0, False, True, c)
        view_step(c)

    def y_wait(c):
        def one(v, carry):
            for k in range(2):
                y_copy(v, k, c).wait_recv()
            return carry

        return one

    def sum_copy(way, step, c, i):
        tiles = pl.ds(17 * c + 9 * i, 9 - i)
        return pltpu.make_async_remote_copy(
            src_ref=sbuf.at[way, step, tiles],
            dst_ref=rbuf.at[way, step, tiles],
            send_sem=r_send.at[way, step, c, i],
            recv_sem=r_recv.at[way, step, c, i],
            device_id=z_to[way],
            device_id_type=MESH,
        )

    def project(pair, target, c, first, last):
        def one(n, carry):
            cols = pl.ds(pl.multiple_of(n * CT, CT), CT)
            block = back[first:last, :, :, cols].reshape((last - first) * 2 * RH, CT)
            got = jnp.dot(bmat[pair, :, first * 128 : last * 128], block, preferred_element_type=F32)
            if first:
                got = got + target[:, cols]
            target[:, cols] = got
            return carry

        lax.fori_loop(STILES[c][0] // 2, STILES[c][1] // 2, one, 0)

    spots = tuple((k, j) for k in range(2) for j in range(4))
    orders = ((0, 1), (1, 0))

    def message(source, way, step, c, i):
        q = orders[way][i]
        at = (64 if step == 0 else (1 - way) * 64) + q * R
        tiles = [source[at + k * H : at + (k + 1) * H, 128 * (4 * c + j) : 128 * (4 * c + j + 1)] for k, j in spots]
        first = 17 * c + 1 + 8 * i
        if step > 1 or (step == 1 and i == 0):
            sum_copy(way, step - 1, c, i).wait_recv()
            base = rbuf[way, step - 1, 17 * c].astype(F32)
            tiles = [tiles[n] + (rbuf[way, step - 1, first + n].astype(F32) + base) for n in range(8)]
        if i == 0:
            mean = sum(tiles[1:], tiles[0]) * 0.125
            sbuf[way, step, 17 * c] = mean.astype(BF)
        mean = sbuf[way, step, 17 * c].astype(F32)
        for n in range(8):
            sbuf[way, step, first + n] = (tiles[n] - mean).astype(BF)
        sum_copy(way, step, c, i).start()

    early = 6
    for c in range(2):
        if c == 0:
            lax.fori_loop(0, V, y_wait(c), 0)
            project(0, own, c, 0, V)
        else:
            lax.fori_loop(0, early, y_wait(c), 0)
            project(0, own, c, 0, early)
            lax.fori_loop(early, V, y_wait(c), 0)
            project(0, own, c, early, V)
        for way in range(2):
            message(own, way, 0, c, 0)
        project(7, part, c, 0, V)
    for step in range(1, 8):
        for c in range(2):
            for i in range(2):
                for way in range(2):
                    message(part, way, step, c, i)
            if step < 7:
                project(7 - step, part, c, 0, V)

    def result(c, q):
        cols = pl.ds(STILES[c][0] * 128, (STILES[c][1] - STILES[c][0]) * 128)
        return pltpu.make_async_copy(obuf.at[q, :, cols], out.at[q, :, cols], o_sem.at[c, q])

    for c in range(2):
        for way in range(2):
            for i in range(2):
                sum_copy(way, 7, c, i).wait_recv()
        for q in range(2):
            bases = [rbuf[way, 7, 17 * c].astype(F32) for way in range(2)]
            for n, (k, j) in enumerate(spots):
                rows = slice(k * H, (k + 1) * H)
                cols = slice(128 * (4 * c + j), 128 * (4 * c + j + 1))
                total = own[q * R + k * H : q * R + (k + 1) * H, cols]
                for way in range(2):
                    total = total + (rbuf[way, 7, 17 * c + 1 + 8 * orders[way].index(q) + n].astype(F32) + bases[way])
                obuf[q, rows, cols] = est[q, rows, cols] * (1.0 + total * share[rows, :])
            result(c, q).start()

    for hop in range(8):
        for c in range(2):
            for way in range(2):
                for i, k in pieces[c]:
                    if hop < 7 or i == 0:
                        hop_copy(way, hop, planes[way][i], k, c).wait_send()
                for i in range(2):
                    if hop > 0 or i == 0:
                        sum_copy(way, hop, c, i).wait_send()
            for side in range(2):
                for copy in halo_copies(hop, side, c):
                    copy.wait_send()
    for c in range(2):
        for v in range(V):
            for k in range(2):
                y_copy(v, k, c).wait_send()
        for q in range(2):
            result(c, q).wait()


def shards(estimate, views, kernel_x, kernel_y, kernel_z, offsets):
    anywhere = pl.BlockSpec(memory_space=pl.ANY)
    dma = pltpu.SemaphoreType.DMA
    return pl.pallas_call(
        body,
        out_shape=jax.ShapeDtypeStruct(estimate.shape, F32),
        in_specs=[anywhere] * 6,
        out_specs=anywhere,
        scratch_shapes=[
            pltpu.VMEM((2, R, NC), F32),
            pltpu.SMEM(kernel_x.shape, F32),
            pltpu.SMEM(kernel_y.shape, F32),
            pltpu.SMEM(kernel_z.shape, F32),
            pltpu.SMEM(offsets.shape, jnp.int32),
            pltpu.VMEM((2, R, NC), F32),
            pltpu.VMEM((R, 128), F32),
            pltpu.VMEM((8, 2, 2, RH, NC), BF),
            pltpu.VMEM((V * 64, NC), F32),
            pltpu.VMEM((V * 64, NC + 2 * PAD), BF),
            pltpu.VMEM((V * 64, NC + 2 * PAD), BF),
            pltpu.VMEM((V, 2, RH, NC), BF),
            pltpu.VMEM((8, V * 64, 256), BF),
            pltpu.VMEM((8, 128, V * 128), BF),
            pltpu.VMEM((V, R, 128), F32),
            pltpu.VMEM((V, R, 128), F32),
            pltpu.VMEM((V, 384, 128), BF),
            pltpu.VMEM((V, 384, 128), BF),
            pltpu.VMEM((V, 2, R, NC), BF),
            pltpu.VMEM((128, NC), F32),
            pltpu.VMEM((128, NC), F32),
            pltpu.VMEM((2, 8, 34, H, 128), BF),
            pltpu.VMEM((2, 8, 34, H, 128), BF),
            dma((2, 8, 2, 3)), dma((2, 8, 2, 3)),
            dma((8, 2, 2, 2, 2)), dma((8, 2, 2, 2, 2)),
            dma((6,)), dma((2, 2)),
            dma((V, 2, 2)), dma((V, 2, 2)),
            dma((2, 8, 2, 2)), dma((2, 8, 2, 2)),
        ],
        compiler_params=pltpu.CompilerParams(
            collective_id=0, has_side_effects=True, vmem_limit_bytes=63 * 1024 * 1024
        ),
        name="rl_step",
    )(estimate, views, kernel_x, kernel_y, kernel_z, offsets)


def solution(mesh):
    in_specs = (P("depth", "tile", None), P(None, "depth", "tile", None), P(), P(), P(), P())
    return jax.shard_map(shards, mesh=mesh, in_specs=in_specs, out_specs=P("depth", "tile", None), check_vma=False)
```

time: 96 us -> 92.5 us (0.964)
  Pallas kernels: 94.1 us -> 90.6 us
    pallas_call x1, Pallas kernels: 94.1 us -> 90.6 us  [shards(): pl.pallas_call(body, out_shape=jax.ShapeDtypeStruct(estimate.shape, F32),...]
where the time goes in v2:
time: 92.5 us; the launch traced here: 92.3 us
  Pallas kernels  90.6 us (98%)
  local copies, waits for them, and re-layouts  1.67 us (2%)
    pallas_call x1, Pallas kernels, shards(): pl.pallas_call(body, out_shape=jax.ShapeDtypeStruct(estimate.shape, F32),...  90.6 us

profile of v2, /device:TPU:32, one launch (start us, length us, event | category | flops | bytes accessed | tf_op | source)
XLA Modules:
  0.0 92.3 jit_solution(7636497140987755273)
XLA Ops:
  0.0 90.6 %rl_step.1 = f32[2,32,1024]{2,1,0:T(8,128)} custom-call(f32[2,32,1024]{2,1,0:T(8,128)} %est_in.1, bf16[8,2,32,1024]{3,2,1,0:T(8,128)(2,1)} %views.1, f32[8,31]{1,0:T(8,128)} %kx_in.1, f32[8,31]{1,0:T(8,128)} %ky_in.1, f32[8,31]{1,0:T(8,128)} %kz_in.1, s32[8]{0:T(128)} %offs_in.1), custom_call_target="tpu_custom_call" | custom-call | tf_op jit(solution)/shard_map/rl_step/pallas_call | solution.py:409
  90.6 1.7 %copy.8 = f32[2,32,1024]{2,1,0:T(8,128)} copy(f32[2,32,1024]{2,1,0:T(8,128)} %rl_step.1) | data formatting | bytes 524288

commit v3 on v2

--- a/solution.py
+++ b/solution.py
@@ -15,7 +15,6 @@
 RH = R + 2 * H
 NC = 1024
 PAD = 128
-CT = 256
 
 
 def place(way, hop):
@@ -26,9 +25,20 @@
     return hop, way
 
 
-GCOLS = ((0, 768), (768, 1024))
-BTILES = ((0, 5), (5, 8))
-STILES = ((0, 4), (4, 8))
+GCOLS = ((0, 640), (640, 1024))
+BTILES = ((0, 4), (4, 8))
+STILES = ((0, 3), (3, 8))
+SPOTS = tuple(tuple((k, n) for k in range(2) for n in range(*ends)) for ends in STILES)
+FIRST = (0, 2 * len(SPOTS[0]) + 1)
+LEAP = 4
+
+
+def parent(leaps, d):
+    return 0 if leaps and d == LEAP else d - 1
+
+
+GLEAPS = (True, False)
+SLEAPS = (False, True)
 
 
 def body(
@@ -48,6 +58,7 @@
     tu = lax.rem(t + nt - 1, nt)
     td = lax.rem(t + 1, nt)
     z_to = ((t, zr), (t, zl))
+    z_far = ((t, lax.rem(b + LEAP, nz)), (t, lax.rem(b + nz - LEAP, nz)))
     t_to = ((tu, b), (td, b))
 
     loads = [
@@ -60,21 +71,22 @@
         load.start()
     barrier = pltpu.get_barrier_semaphore()
     corners = tuple((x, z) for x in (tu, td) for z in (zr, zl))
-    for device in z_to + t_to + corners:
+    for device in z_to + z_far + t_to + corners:
         pl.semaphore_signal(barrier, inc=1, device_id=device, device_id_type=MESH)
 
-    def hop_copy(way, hop, q, k, c):
-        pair, side = place(way, hop)
-        pair2, side2 = place(way, hop + 1)
+    def hop_copy(way, d, q, k, c):
+        source = parent(GLEAPS[c], d)
+        pair, side = place(way, source)
+        pair2, side2 = place(way, d)
         rows = pl.ds(H + k * H, H) if c == 0 else pl.ds(H, R)
         cols = pl.ds(GCOLS[c][0], GCOLS[c][1] - GCOLS[c][0])
         sem = k if c == 0 else 2
         return pltpu.make_async_remote_copy(
             src_ref=gath.at[pair, side, q, rows, cols],
             dst_ref=gath.at[pair2, side2, q, rows, cols],
-            send_sem=g_send.at[way, hop, q, sem],
-            recv_sem=g_recv.at[way, hop, q, sem],
-            device_id=z_to[way],
+            send_sem=g_send.at[way, d - 1, q, sem],
+            recv_sem=g_recv.at[way, d - 1, q, sem],
+            device_id=(z_to if d - source == 1 else z_far)[way],
             device_id_type=MESH,
         )
 
@@ -108,11 +120,13 @@
     pieces = (((0, 0), (0, 1), (1, 0), (1, 1)), ((0, 0), (1, 0)))
     loads[0].wait()
     gath[0, 0, :, H : H + R, :] = est[...].astype(BF)
-    pl.semaphore_wait(barrier, 8)
+    pl.semaphore_wait(barrier, 10)
     for c in range(2):
-        for i, k in pieces[c]:
-            for way in range(2):
-                hop_copy(way, 0, planes[way][i], k, c).start()
+        for d in range(8, 0, -1):
+            if parent(GLEAPS[c], d) == 0:
+                for i, k in pieces[c]:
+                    for way in range(2):
+                        hop_copy(way, d, planes[way][i], k, c).start()
         for copy in halo_copies(0, 0, c):
             copy.start()
     for load in loads[1:5]:
@@ -190,18 +204,18 @@
 
     def forward(pair, begin, end, chunk):
         def one(n, carry):
-            cols = pl.ds(pl.multiple_of(n * CT, CT), CT)
-            block = gath[pair, :, :, :, cols].reshape(4 * RH, CT)
+            cols = pl.ds(pl.multiple_of(n * 128, 128), 128)
+            block = gath[pair, :, :, :, cols].reshape(4 * RH, 128)
             got = jnp.dot(amat[pair], block, preferred_element_type=F32)
             if not begin:
                 got = got + acc[:, cols]
             if end:
-                blur[:, pl.ds(pl.multiple_of(n * CT + PAD, PAD), CT)] = got.astype(BF)
+                blur[:, pl.ds(pl.multiple_of(n * 128 + PAD, PAD), 128)] = got.astype(BF)
             else:
                 acc[:, cols] = got
             return carry
 
-        lax.fori_loop(GCOLS[chunk][0] // CT, GCOLS[chunk][1] // CT, one, 0)
+        lax.fori_loop(GCOLS[chunk][0] // 128, GCOLS[chunk][1] // 128, one, 0)
 
     for ref in (blur, corr):
         ref[:, :PAD] = jnp.zeros((ref.shape[0], PAD), BF)
@@ -217,27 +231,38 @@
             for copy in halo_copies(pair, side, c):
                 copy.wait_recv()
 
-    for hop in range(1, 8):
-        for c in range(2):
-            for i, k in pieces[c]:
-                for way in range(2):
-                    q = planes[way][i]
-                    hop_copy(way, hop - 1, q, k, c).wait_recv()
-                    if hop < 7 or i == 0:
-                        hop_copy(way, hop, q, k, c).start()
-                    if hop == 7 and i == 0:
-                        for kk in (k,) if c == 0 else (0, 1):
-                            halo_copy(0, 1, q, kk, c).start()
+    def arrive(c, d):
+        for i, k in pieces[c]:
+            for way in range(2):
+                q = planes[way][i]
+                if d < 8 or i == 0:
+                    hop_copy(way, d, q, k, c).wait_recv()
+                if d < 7 and parent(GLEAPS[c], d + 1) == d or d == 7 and i == 0:
+                    hop_copy(way, d + 1, q, k, c).start()
+                if d == 7 and i == 0:
+                    for kk in (k,) if c == 0 else (0, 1):
+                        halo_copy(0, 1, q, kk, c).start()
+        if d < 8:
             for side in range(2):
-                for copy in halo_copies(hop, side, c):
+                for copy in halo_copies(d, side, c):
                     copy.start()
-        mats(hop)
-        if hop >= 2:
-            for c in range(2):
-                halos(hop - 1, c)
-                forward(hop - 1, hop == 2, False, c)
-    mats(0)
-    loads[5].wait()
+
+    ready = set()
+    waiting = []
+
+    def combine(c, d):
+        pair = d % 8
+        if pair not in ready:
+            ready.add(pair)
+            mats(pair)
+        halos(pair, c)
+        forward(pair, d == 1, d == 8, c)
+
+    def gather(c, d):
+        arrive(c, d)
+        waiting.append((c, d))
+        if len(waiting) > 2:
+            combine(*waiting.pop(0))
 
     row = lax.broadcasted_iota(jnp.int32, (2 * R, 128), 0)
     row = jnp.where(row >= R, row - R, row) + t * R
@@ -270,7 +295,7 @@
         for i, n in enumerate(tiles):
             back[v, :, H : H + R, n * 128 : (n + 1) * 128] = spread[i * 64 : (i + 1) * 64].reshape(2, R, 128)
 
-    def view_step(c):
+    def view_step(c, first, last):
         def step(i, carry):
             for v in (2 * i, 2 * i + 1):
                 view_work(v, c)
@@ -279,18 +304,7 @@
                     y_copy(v, k, c).start()
             return carry
 
-        lax.fori_loop(0, V // 2, step, 0)
-
-    for c in range(2):
-        halos(7, c)
-        forward(7, False, False, c)
-        for i, k in pieces[c]:
-            if i == 0:
-                for way in range(2):
-                    hop_copy(way, 7, planes[way][0], k, c).wait_recv()
-        halos(0, c)
-        forward(0, False, True, c)
-        view_step(c)
+        lax.fori_loop(first // 2, last // 2, step, 0)
 
     def y_wait(c):
         def one(v, carry):
@@ -300,100 +314,125 @@
 
         return one
 
-    def sum_copy(way, step, c, i):
-        tiles = pl.ds(17 * c + 9 * i, 9 - i)
+    def sum_copy(way, d, c, i):
+        count = len(SPOTS[c])
+        tiles = pl.ds(FIRST[c] + (count + 1) * i, count + 1 - i)
         return pltpu.make_async_remote_copy(
-            src_ref=sbuf.at[way, step, tiles],
-            dst_ref=rbuf.at[way, step, tiles],
-            send_sem=r_send.at[way, step, c, i],
-            recv_sem=r_recv.at[way, step, c, i],
-            device_id=z_to[way],
+            src_ref=sbuf.at[way, d - 1, tiles],
+            dst_ref=rbuf.at[way, d - 1, tiles],
+            send_sem=r_send.at[way, d - 1, c, i],
+            recv_sem=r_recv.at[way, d - 1, c, i],
+            device_id=(z_to if d - parent(SLEAPS[c], d) == 1 else z_far)[way],
             device_id_type=MESH,
         )
 
     def project(pair, target, c, first, last):
         def one(n, carry):
-            cols = pl.ds(pl.multiple_of(n * CT, CT), CT)
-            block = back[first:last, :, :, cols].reshape((last - first) * 2 * RH, CT)
+            cols = pl.ds(pl.multiple_of(n * 128, 128), 128)
+            block = back[first:last, :, :, cols].reshape((last - first) * 2 * RH, 128)
             got = jnp.dot(bmat[pair, :, first * 128 : last * 128], block, preferred_element_type=F32)
             if first:
                 got = got + target[:, cols]
             target[:, cols] = got
             return carry
 
-        lax.fori_loop(STILES[c][0] // 2, STILES[c][1] // 2, one, 0)
-
-    spots = tuple((k, j) for k in range(2) for j in range(4))
+        lax.fori_loop(STILES[c][0], STILES[c][1], one, 0)
+
     orders = ((0, 1), (1, 0))
 
-    def message(source, way, step, c, i):
+    def message(way, d, c, i):
         q = orders[way][i]
-        at = (64 if step == 0 else (1 - way) * 64) + q * R
-        tiles = [source[at + k * H : at + (k + 1) * H, 128 * (4 * c + j) : 128 * (4 * c + j + 1)] for k, j in spots]
-        first = 17 * c + 1 + 8 * i
-        if step > 1 or (step == 1 and i == 0):
-            sum_copy(way, step - 1, c, i).wait_recv()
-            base = rbuf[way, step - 1, 17 * c].astype(F32)
-            tiles = [tiles[n] + (rbuf[way, step - 1, first + n].astype(F32) + base) for n in range(8)]
+        source = own if d == 8 else part
+        at = (64 if d == 8 else (1 - way) * 64) + q * R
+        count = len(SPOTS[c])
+        tiles = [source[at + k * H : at + (k + 1) * H, 128 * n : 128 * (n + 1)] for k, n in SPOTS[c]]
+        first = FIRST[c] + 1 + count * i
+        if d < 8 and parent(SLEAPS[c], d + 1) == d and (d < 7 or i == 0):
+            sum_copy(way, d + 1, c, i).wait_recv()
+            base = rbuf[way, d, FIRST[c]].astype(F32)
+            tiles = [tiles[n] + (rbuf[way, d, first + n].astype(F32) + base) for n in range(count)]
         if i == 0:
-            mean = sum(tiles[1:], tiles[0]) * 0.125
-            sbuf[way, step, 17 * c] = mean.astype(BF)
-        mean = sbuf[way, step, 17 * c].astype(F32)
-        for n in range(8):
-            sbuf[way, step, first + n] = (tiles[n] - mean).astype(BF)
-        sum_copy(way, step, c, i).start()
-
-    early = 6
-    for c in range(2):
-        if c == 0:
-            lax.fori_loop(0, V, y_wait(c), 0)
-            project(0, own, c, 0, V)
-        else:
-            lax.fori_loop(0, early, y_wait(c), 0)
-            project(0, own, c, 0, early)
-            lax.fori_loop(early, V, y_wait(c), 0)
-            project(0, own, c, early, V)
-        for way in range(2):
-            message(own, way, 0, c, 0)
-        project(7, part, c, 0, V)
-    for step in range(1, 8):
-        for c in range(2):
-            for i in range(2):
-                for way in range(2):
-                    message(part, way, step, c, i)
-            if step < 7:
-                project(7 - step, part, c, 0, V)
+            mean = sum(tiles[1:], tiles[0]) * (1.0 / count)
+            sbuf[way, d - 1, FIRST[c]] = mean.astype(BF)
+        mean = sbuf[way, d - 1, FIRST[c]].astype(F32)
+        for n in range(count):
+            sbuf[way, d - 1, first + n] = (tiles[n] - mean).astype(BF)
+        sum_copy(way, d, c, i).start()
+
+    sequence = ((8, 7, 6, 5, 4, 3, 2, 1), (8, 3, 7, 2, 6, 1, 5, 4))
+
+    def send_sums(c, d):
+        for i in range(2 if d < 8 else 1):
+            for way in range(2):
+                message(way, d, c, i)
+        if d != sequence[c][-1]:
+            project(sequence[c][sequence[c].index(d) + 1], part, c, 0, V)
 
     def result(c, q):
         cols = pl.ds(STILES[c][0] * 128, (STILES[c][1] - STILES[c][0]) * 128)
         return pltpu.make_async_copy(obuf.at[q, :, cols], out.at[q, :, cols], o_sem.at[c, q])
 
-    for c in range(2):
-        for way in range(2):
-            for i in range(2):
-                sum_copy(way, 7, c, i).wait_recv()
+    def finish(c):
+        count = len(SPOTS[c])
+        last = [d for d in range(1, 9) if parent(SLEAPS[c], d) == 0]
+        for d in last:
+            for way in range(2):
+                for i in range(2):
+                    sum_copy(way, d, c, i).wait_recv()
         for q in range(2):
-            bases = [rbuf[way, 7, 17 * c].astype(F32) for way in range(2)]
-            for n, (k, j) in enumerate(spots):
+            base = sum(rbuf[way, d - 1, FIRST[c]].astype(F32) for way in range(2) for d in last)
+            for m, (k, n) in enumerate(SPOTS[c]):
                 rows = slice(k * H, (k + 1) * H)
-                cols = slice(128 * (4 * c + j), 128 * (4 * c + j + 1))
-                total = own[q * R + k * H : q * R + (k + 1) * H, cols]
+                cols = slice(128 * n, 128 * (n + 1))
+                total = own[q * R + k * H : q * R + (k + 1) * H, cols] + base
                 for way in range(2):
-                    total = total + (rbuf[way, 7, 17 * c + 1 + 8 * orders[way].index(q) + n].astype(F32) + bases[way])
+                    for d in last:
+                        total = total + rbuf[way, d - 1, FIRST[c] + 1 + count * orders[way].index(q) + m].astype(F32)
                 obuf[q, rows, cols] = est[q, rows, cols] * (1.0 + total * share[rows, :])
             result(c, q).start()
 
-    for hop in range(8):
+    for c, d in ((0, 1), (1, 1), (0, 4), (0, 2), (1, 2), (0, 5), (0, 3), (1, 3), (0, 6), (1, 4), (0, 7), (1, 5)):
+        gather(c, d)
+    while any(c == 0 for c, d in waiting):
+        combine(*waiting.pop(0))
+    loads[5].wait()
+    arrive(0, 8)
+    combine(0, 8)
+    view_step(0, 0, 4)
+    gather(1, 6)
+    view_step(0, 4, 8)
+    gather(1, 7)
+    while waiting:
+        combine(*waiting.pop(0))
+    lax.fori_loop(0, V, y_wait(0), 0)
+    project(0, own, 0, 0, V)
+    send_sums(0, 8)
+    arrive(1, 8)
+    combine(1, 8)
+    view_step(1, 0, 8)
+    send_sums(0, 7)
+    early = 6
+    lax.fori_loop(0, early, y_wait(1), 0)
+    project(0, own, 1, 0, early)
+    lax.fori_loop(early, V, y_wait(1), 0)
+    project(0, own, 1, early, V)
+    for c, d in (
+        (1, 8), (1, 3), (0, 6), (1, 7), (1, 2), (0, 5), (1, 6), (1, 1), (0, 4), (1, 5), (0, 3), (1, 4), (0, 2), (0, 1),
+    ):
+        send_sums(c, d)
+    for c in range(2):
+        finish(c)
+
+    for d in range(1, 9):
         for c in range(2):
             for way in range(2):
                 for i, k in pieces[c]:
-                    if hop < 7 or i == 0:
-                        hop_copy(way, hop, planes[way][i], k, c).wait_send()
-                for i in range(2):
-                    if hop > 0 or i == 0:
-                        sum_copy(way, hop, c, i).wait_send()
+                    if d < 8 or i == 0:
+                        hop_copy(way, d, planes[way][i], k, c).wait_send()
+                for i in range(2 if d < 8 else 1):
+                    sum_copy(way, d, c, i).wait_send()
             for side in range(2):
-                for copy in halo_copies(hop, side, c):
+                for copy in halo_copies(d % 8, side, c):
                     copy.wait_send()
     for c in range(2):
         for v in range(V):

time: 92.5 us -> 108 us (1.17)
  the two profiles are of different devices: /device:TPU:32 before, /device:TPU:64 now
where the time goes in v3:
time: 108 us
  Pallas kernels  107 us (99%)
  local copies, waits for them, and re-layouts  1.67 us (2%)
    pallas_call x1, Pallas kernels, shards(): pl.pallas_call(body, out_shape=jax.ShapeDtypeStruct(estimate.shape, F32),...  107 us

profile of v3, /device:TPU:64, one launch (start us, length us, event | category | flops | bytes accessed | tf_op | source)
XLA Modules:
  0.0 108.3 jit_solution(7938062602415790945)
XLA Ops:
  0.0 106.6 %rl_step.1 = f32[2,32,1024]{2,1,0:T(8,128)} custom-call(f32[2,32,1024]{2,1,0:T(8,128)} %est_in.1, bf16[8,2,32,1024]{3,2,1,0:T(8,128)(2,1)} %views.1, f32[8,31]{1,0:T(8,128)} %kx_in.1, f32[8,31]{1,0:T(8,128)} %ky_in.1, f32[8,31]{1,0:T(8,128)} %kz_in.1, s32[8]{0:T(128)} %offs_in.1), custom_call_target="tpu_custom_call" | custom-call | tf_op jit(solution)/shard_map/rl_step/pallas_call | solution.py:448
  106.6 1.7 %copy.8 = f32[2,32,1024]{2,1,0:T(8,128)} copy(f32[2,32,1024]{2,1,0:T(8,128)} %rl_step.1) | data formatting | bytes 524288

commit v4 on v2

--- a/solution.py
+++ b/solution.py
@@ -29,6 +29,9 @@
 GCOLS = ((0, 768), (768, 1024))
 BTILES = ((0, 5), (5, 8))
 STILES = ((0, 4), (4, 8))
+
+SINGLY = ((0, 1), (7, 0), (7, 1))
+DIAGONAL = ((0, 1),)
 
 
 def body(
@@ -81,10 +84,12 @@
     def halo_copy(pair, side, q, k, c):
         src, dst = ((H, H + R), (R, 0))[k]
         cols = pl.ds(GCOLS[c][0], GCOLS[c][1] - GCOLS[c][0])
-        if (pair, side) == (0, 1):
-            way = 1 - q
-            pair2, side2 = place(way, 7)
-            device = ((tu, td)[k], (zr, zl)[way])
+        if (pair, side) in SINGLY:
+            pair2, side2, device = pair, side, t_to[k]
+            if (pair, side) in DIAGONAL:
+                way = side if pair else 1 - q
+                pair2, side2 = place(way, (pair or 8) - 1)
+                device = ((tu, td)[k], (zr, zl)[way])
             source = gath.at[pair2, side2, q, pl.ds(src, H), cols]
             target = gath.at[pair, side, q, pl.ds(dst, H), cols]
         else:
@@ -101,7 +106,7 @@
         )
 
     def halo_copies(pair, side, c):
-        qs = (0, 1) if (pair, side) == (0, 1) else (0,)
+        qs = (0, 1) if (pair, side) in SINGLY else (0,)
         return [halo_copy(pair, side, q, k, c) for q in qs for k in range(2)]
 
     planes = ((1, 0), (0, 1))
@@ -203,9 +208,8 @@
 
         lax.fori_loop(GCOLS[chunk][0] // CT, GCOLS[chunk][1] // CT, one, 0)
 
-    for ref in (blur, corr):
-        ref[:, :PAD] = jnp.zeros((ref.shape[0], PAD), BF)
-        ref[:, PAD + NC :] = jnp.zeros((ref.shape[0], PAD), BF)
+    blur[:, :PAD] = jnp.zeros((V * 64, PAD), BF)
+    blur[:, PAD + NC :] = jnp.zeros((V * 64, PAD), BF)
     rid = lax.broadcasted_iota(jnp.int32, (R, 128), 0) + t * R
     seen_by = jnp.zeros((R, 128), F32)
     for v in range(V):
@@ -225,12 +229,15 @@
                     hop_copy(way, hop - 1, q, k, c).wait_recv()
                     if hop < 7 or i == 0:
                         hop_copy(way, hop, q, k, c).start()
-                    if hop == 7 and i == 0:
-                        for kk in (k,) if c == 0 else (0, 1):
+                    for kk in (k,) if c == 0 else (0, 1):
+                        if hop == 7 and i == 0:
                             halo_copy(0, 1, q, kk, c).start()
-            for side in range(2):
-                for copy in halo_copies(hop, side, c):
-                    copy.start()
+                        if hop == 7:
+                            halo_copy(7, way, q, kk, c).start()
+            if hop < 7:
+                for side in range(2):
+                    for copy in halo_copies(hop, side, c):
+                        copy.start()
         mats(hop)
         if hop >= 2:
             for c in range(2):
@@ -260,12 +267,20 @@
         tiles = range(*BTILES[c])
         lhs = jnp.concatenate([blur[rows, n * 128 : n * 128 + 384] for n in tiles], axis=0)
         blurred = jnp.dot(lhs, yfwd[v], preferred_element_type=F32)
+        none = jnp.zeros((2 * R, 128), BF)
+        fixes = {-1: none, NC // 128: none}
+        if c == 1:
+            fixes[tiles[0] - 2] = corr[rows, :128]
+            fixes[tiles[0] - 1] = corr[rows, 128:]
         for i, n in enumerate(tiles):
             seen = vbuf[v, :, :, n * 128 : (n + 1) * 128].astype(F32).reshape(2 * R, 128)
             ratio = seen / blurred[i * 64 : (i + 1) * 64]
-            corr[rows, PAD + n * 128 : PAD + (n + 1) * 128] = jnp.where(inside, ratio - 1.0, 0.0).astype(BF)
+            fixes[n] = jnp.where(inside, ratio - 1.0, 0.0).astype(BF)
+        if c == 0:
+            corr[rows, :128] = fixes[tiles[-1] - 1]
+            corr[rows, 128:] = fixes[tiles[-1]]
         tiles = range(*STILES[c])
-        lhs = jnp.concatenate([corr[rows, n * 128 : n * 128 + 384] for n in tiles], axis=0)
+        lhs = jnp.concatenate([jnp.concatenate([fixes[n - 1], fixes[n], fixes[n + 1]], axis=1) for n in tiles], axis=0)
         spread = jnp.dot(lhs, ybwd[v], preferred_element_type=F32).astype(BF)
         for i, n in enumerate(tiles):
             back[v, :, H : H + R, n * 128 : (n + 1) * 128] = spread[i * 64 : (i + 1) * 64].reshape(2, R, 128)
@@ -380,7 +395,7 @@
                 total = own[q * R + k * H : q * R + (k + 1) * H, cols]
                 for way in range(2):
                     total = total + (rbuf[way, 7, 17 * c + 1 + 8 * orders[way].index(q) + n].astype(F32) + bases[way])
-                obuf[q, rows, cols] = est[q, rows, cols] * (1.0 + total * share[rows, :])
+                obuf[q, rows, cols] = total * share[rows, :]
             result(c, q).start()
 
     for hop in range(8):
@@ -406,7 +421,7 @@
 def shards(estimate, views, kernel_x, kernel_y, kernel_z, offsets):
     anywhere = pl.BlockSpec(memory_space=pl.ANY)
     dma = pltpu.SemaphoreType.DMA
-    return pl.pallas_call(
+    change = pl.pallas_call(
         body,
         out_shape=jax.ShapeDtypeStruct(estimate.shape, F32),
         in_specs=[anywhere] * 6,
@@ -422,7 +437,7 @@
             pltpu.VMEM((8, 2, 2, RH, NC), BF),
             pltpu.VMEM((V * 64, NC), F32),
             pltpu.VMEM((V * 64, NC + 2 * PAD), BF),
-            pltpu.VMEM((V * 64, NC + 2 * PAD), BF),
+            pltpu.VMEM((V * 64, 256), BF),
             pltpu.VMEM((V, 2, RH, NC), BF),
             pltpu.VMEM((8, V * 64, 256), BF),
             pltpu.VMEM((8, 128, V * 128), BF),
@@ -446,6 +461,7 @@
         ),
         name="rl_step",
     )(estimate, views, kernel_x, kernel_y, kernel_z, offsets)
+    return estimate * (1.0 + change)
 
 
 def solution(mesh):

time: 92.5 us -> 91.9 us (level)
  other arithmetic: 0 us -> 1.68 us
  local copies, waits for them, and re-layouts: 1.67 us -> 0.01 us
    mul x0 -> x1, other arithmetic: none -> 1.68 us  [shards(): return estimate * (1.0 + change)]
    unnamed x1 -> x2, local copies, waits for them, and re-layouts: 1.67 us -> 0.01 us
where the time goes in v4:
time: 91.9 us; the launch traced here: 91.7 us
  Pallas kernels  90 us (98%)
  other arithmetic  1.68 us (2%)
    pallas_call x1, Pallas kernels, shards(): pl.pallas_call(body, out_shape=jax.ShapeDtypeStruct(estimate.shape, F32),...  90 us

profile of v4, /device:TPU:32, one launch (start us, length us, event | category | flops | bytes accessed | tf_op | source)
XLA Modules:
  0.0 91.7 jit_solution(13278423039460940585)
XLA Ops:
  0.0 0.0 copy-start
  0.0 90.0 %rl_step.1 = f32[2,32,1024]{2,1,0:T(8,128)} custom-call(f32[2,32,1024]{2,1,0:T(8,128)} %est_in.1, bf16[8,2,32,1024]{3,2,1,0:T(8,128)(2,1)} %views.1, f32[8,31]{1,0:T(8,128)} %kx_in.1, f32[8,31]{1,0:T(8,128)} %ky_in.1, f32[8,31]{1,0:T(8,128)} %kz_in.1, s32[8]{0:T(128)} %offs_in.1), custom_call_target="tpu_custom_call" | custom-call | tf_op jit(solution)/shard_map/rl_step/pallas_call | solution.py:424
  90.0 0.0 copy-done
  90.1 1.7 %add_multiply_fusion = f32[2,32,1024]{2,1,0:T(8,128)} fusion(f32[2,32,1024]{2,1,0:T(8,128)S(1)} %copy-done, f32[2,32,1024]{2,1,0:T(8,128)} %rl_step.1), kind=kLoop, calls=%fused_computation | loop fusion | flops 131072 | bytes 786432 | tf_op jit(solution)/shard_map/mul | solution.py:464
Async XLA Ops:
  0.0 90.1 %copy-start = (f32[2,32,1024]{2,1,0:T(8,128)S(1)}, f32[2,32,1024]{2,1,0:T(8,128)}, u32[]{:S(2)}) copy-start(f32[2,32,1024]{2,1,0:T(8,128)} %est_in.1) | copy-start | bytes 786436

commit v5 on v4

--- a/solution.py
+++ b/solution.py
@@ -59,12 +59,13 @@
             ((est_in, est), (kx_in, kx), (ky_in, ky), (kz_in, kz), (offs_in, offs), (views, vbuf))
         )
     ]
-    for load in loads:
-        load.start()
+    loads[0].start()
     barrier = pltpu.get_barrier_semaphore()
     corners = tuple((x, z) for x in (tu, td) for z in (zr, zl))
     for device in z_to + t_to + corners:
         pl.semaphore_signal(barrier, inc=1, device_id=device, device_id_type=MESH)
+    for load in loads[1:]:
+        load.start()
 
     def hop_copy(way, hop, q, k, c):
         pair, side = place(way, hop)

time: 91.9 us -> 92 us (level)
  no operation moved by 1% of the time
where the time goes in v5:
time: 92 us; the launch traced here: 91.8 us
  Pallas kernels  90.1 us (98%)
  other arithmetic  1.68 us (2%)
    pallas_call x1, Pallas kernels, shards(): pl.pallas_call(body, out_shape=jax.ShapeDtypeStruct(estimate.shape, F32),...  90.1 us

profile of v5, /device:TPU:32, one launch (start us, length us, event | category | flops | bytes accessed | tf_op | source)
XLA Modules:
  0.0 91.8 jit_solution(5339558598675729142)
XLA Ops:
  0.0 0.0 copy-start
  0.0 90.1 %rl_step.1 = f32[2,32,1024]{2,1,0:T(8,128)} custom-call(f32[2,32,1024]{2,1,0:T(8,128)} %est_in.1, bf16[8,2,32,1024]{3,2,1,0:T(8,128)(2,1)} %views.1, f32[8,31]{1,0:T(8,128)} %kx_in.1, f32[8,31]{1,0:T(8,128)} %ky_in.1, f32[8,31]{1,0:T(8,128)} %kz_in.1, s32[8]{0:T(128)} %offs_in.1), custom_call_target="tpu_custom_call" | custom-call | tf_op jit(solution)/shard_map/rl_step/pallas_call | solution.py:425
  90.1 0.0 copy-done
  90.1 1.7 %add_multiply_fusion = f32[2,32,1024]{2,1,0:T(8,128)} fusion(f32[2,32,1024]{2,1,0:T(8,128)S(1)} %copy-done, f32[2,32,1024]{2,1,0:T(8,128)} %rl_step.1), kind=kLoop, calls=%fused_computation | loop fusion | flops 131072 | bytes 786432 | tf_op jit(solution)/shard_map/mul | solution.py:465
Async XLA Ops:
  0.0 90.1 %copy-start = (f32[2,32,1024]{2,1,0:T(8,128)S(1)}, f32[2,32,1024]{2,1,0:T(8,128)}, u32[]{:S(2)}) copy-start(f32[2,32,1024]{2,1,0:T(8,128)} %est_in.1) | copy-start | bytes 786436
